TPU v7x, 32 devices: a whole 2x2x4 slice. The times are simulated.
32 devices in a mesh: dp: 16 (over z, y, core), expert: 2 (over x).
Axes of the slice: x: 2, y: 2, z: 4, core: 2. Of those that a mesh axis runs over, the one named last changes fastest.
Arguments:
- tokens: bfloat16 [4096, 2048], P(('dp', 'expert')), may hold values from -6 to 6
- cotangent: bfloat16 [4096, 2048], P(('dp', 'expert')), may hold values from -6 to 6
- expert_ids: int32 [4096, 8], P(('dp', 'expert')), may hold values from 0 to 127, as said below
- route_weights: float32 [4096, 8], P(('dp', 'expert')), may hold values from 0.1 to 1
- join_groups: int32 [16], replicated, may hold values from 0 to 1
- w_gate: bfloat16 [2048, 1024], P('dp', 'expert'), may hold values from -0.125 to 0.125
- w_up: bfloat16 [2048, 1024], P('dp', 'expert'), may hold values from -0.125 to 0.125
- w_down: bfloat16 [2048, 1024], P('dp', 'expert'), may hold values from -0.1875 to 0.1875
Outputs:
- mixed: bfloat16 [4096, 2048], P(('dp', 'expert'))
- grad_gate: bfloat16 [2048, 1024], P('dp', 'expert')
- grad_up: bfloat16 [2048, 1024], P('dp', 'expert')
- grad_down: bfloat16 [2048, 1024], P('dp', 'expert')
Inputs may be any that keep to these rules, and one draw needn't show every extreme that they name: `expert_ids`: each row names 8 different experts; the rows of one device name expert 0 at most 16 times, and the rows of some device exactly 16 times.
All inputs are finite; a program needn't handle non-finite values.
Results may differ from a plain program's by a relative error of at most 0.014.
Values may be sent and summed in bfloat16 or wider, within the bound.
A program may use at most 64 MiB of HBM per device.

v0:
```python
import jax
import jax.numpy as jnp
from jax import lax
from jax.sharding import PartitionSpec as P


def per_device(tokens, cotangent, expert_ids, route_weights, join_groups, w_gate, w_up, w_down):
    highest = lax.Precision.HIGHEST
    tok_count = tokens.shape[0]
    slot_count = tok_count // 8
    slice_width = w_gate.shape[1]
    chosen_mask = expert_ids == 0
    routed = jnp.any(chosen_mask, -1)
    weight = jnp.sum(jnp.where(chosen_mask, route_weights, 0.0), -1)
    places = jnp.cumsum(routed.astype(jnp.int32)) - 1
    slot_ids = jnp.arange(slot_count, dtype=jnp.int32)
    chooser = ((places[None, :] == slot_ids[:, None]) & routed[None, :]).astype(jnp.float32)
    chooser_half = chooser.astype(jnp.bfloat16)
    picked_local = jnp.dot(chooser_half, tokens, preferred_element_type=jnp.float32).astype(
        jnp.bfloat16
    )
    picked = lax.all_gather(picked_local, "expert", axis=0, tiled=True)
    gate_acts = jnp.dot(
        picked, lax.all_gather(w_gate, "dp", axis=0, tiled=True), preferred_element_type=jnp.float32
    )
    up_acts = jnp.dot(
        picked, lax.all_gather(w_up, "dp", axis=0, tiled=True), preferred_element_type=jnp.float32
    )
    hidden = (jax.nn.silu(gate_acts) * up_acts).astype(jnp.bfloat16)
    trans_dims = (((1,), (1,)), ((), ()))
    full_down = lax.all_gather(w_down, "dp", axis=0, tiled=True)
    partial_out = lax.dot_general(hidden, full_down, trans_dims, preferred_element_type=jnp.float32)
    out_rows = lax.psum_scatter(
        partial_out.astype(jnp.bfloat16), "expert", scatter_dimension=0, tiled=True
    ).astype(jnp.float32)
    placed = lax.dot_general(
        chooser,
        out_rows,
        (((0,), (0,)), ((), ())),
        precision=highest,
        preferred_element_type=jnp.float32,
    )
    mixed = (placed * weight[:, None]).astype(jnp.bfloat16)
    scaled = cotangent.astype(jnp.float32) * weight[:, None]
    dpicked_local = jnp.dot(
        chooser, scaled, precision=highest, preferred_element_type=jnp.float32
    ).astype(jnp.bfloat16)
    dpicked = lax.all_gather(dpicked_local, "expert", axis=0, tiled=True)
    hidden_grad = jnp.dot(dpicked, full_down, preferred_element_type=jnp.float32)
    sigma_gate = jax.nn.sigmoid(gate_acts)
    dgate = (hidden_grad * up_acts * sigma_gate * (1.0 + gate_acts * (1.0 - sigma_gate))).astype(
        jnp.bfloat16
    )
    dup = (hidden_grad * gate_acts * sigma_gate).astype(jnp.bfloat16)
    group_total = lax.axis_size("dp")
    mine = jnp.arange(group_total, dtype=jnp.int32) == lax.axis_index("dp")
    active = 1.0 - jnp.sum(jnp.where(mine, join_groups, 0)).astype(jnp.float32)
    col_dims = (((0,), (0,)), ((), ()))

    def term_of(left, right):
        return active * lax.dot_general(left, right, col_dims, preferred_element_type=jnp.float32)

    summed = lax.psum_scatter(
        jnp.concatenate(
            [term_of(picked, dgate), term_of(picked, dup), term_of(dpicked, hidden)], axis=1
        ),
        "dp",
        scatter_dimension=0,
        tiled=True,
    )
    grad_gate = summed[:, :slice_width]
    grad_up = summed[:, slice_width : 2 * slice_width]
    grad_down = summed[:, 2 * slice_width :]
    return (
        mixed,
        grad_gate.astype(jnp.bfloat16),
        grad_up.astype(jnp.bfloat16),
        grad_down.astype(jnp.bfloat16),
    )


def solution(mesh):
    in_specs = (
        P(("dp", "expert"), None),
        P(("dp", "expert"), None),
        P(("dp", "expert"), None),
        P(("dp", "expert"), None),
        P(),
        P("dp", "expert"),
        P("dp", "expert"),
        P("dp", "expert"),
    )
    out_specs = (P(("dp", "expert"), None), P("dp", "expert"), P("dp", "expert"), P("dp", "expert"))
    return jax.shard_map(
        per_device, mesh=mesh, in_specs=in_specs, out_specs=out_specs, check_vma=False
    )
```

profile of v0, /device:TPU:0, one launch (start us, length us, event | category | flops | bytes accessed | tf_op | source)
XLA Modules:
  0.0 300.2 jit_solution(16604740441010829208)
XLA Ops:
  7.2 0.0 copy-start
  7.2 0.0 all-gather.4.cloned.1.call-start
  7.2 0.7 all-gather.4.cloned.1.call-update
  7.9 0.0 all-gather.6.cloned.1.call-start
  8.0 0.7 all-gather.6.cloned.1.call-update
  8.7 0.0 all-gather.8.cloned.1.call-start
  8.7 0.7 all-gather.8.cloned.1.call-update
  9.4 0.0 reduce-scatter.3.cloned.1.call-start
  9.5 1.3 fusion.15
  11.4 0.7 select_reduce_fusion
  12.1 0.1 copy.16
  12.3 0.2 reduce-window.8
  12.4 0.1 add_reduce_fusion
  12.5 1.6 convolution_convert_fusion.1
  14.2 5.9 %all_gather.19 = bf16[32,2048]{1,0:T(8,128)(2,1)S(1)} all-gather(bf16[16,2048]{1,0:T(8,128)(2,1)S(1)} %convolution_convert_fusion.1), channel_id=1, replica_groups=mesh['dp'=16,'expert'=2] {'expert'}, dimensions={0}, use_global_device_ids=true | all-gather | bytes 196608 | tf_op jit(solution)/shard_map/all_gather | solution.py:48
  20.0 0.0 copy-done
  20.0 0.2 convolution_convert_fusion.2
  20.2 4.9 %all_gather.15 = bf16[32,2048]{1,0:T(8,128)(2,1)S(1)} all-gather(bf16[16,2048]{1,0:T(8,128)(2,1)S(1)} %convolution_convert_fusion.2), channel_id=1, replica_groups=mesh['dp'=16,'expert'=2] {'expert'}, dimensions={0}, use_global_device_ids=true | all-gather | bytes 196608 | tf_op jit(solution)/shard_map/all_gather | solution.py:22
  25.1 29.2 %all-gather.4.cloned.1.call-done = bf16[2048,512]{1,0:T(8,128)(2,1)} async-done(((bf16[128,512]{1,0:T(8,128)(2,1)}), bf16[2048,512]{1,0:T(8,128)(2,1)}) %all-gather.4.cloned.1.call-update) | async-done | bytes 2097168 | tf_op jit(solution)/shard_map/all_gather | solution.py:24
  54.4 2.0 fusion.19
  56.4 40.3 %all-gather.6.cloned.1.call-done = bf16[2048,512]{1,0:T(8,128)(2,1)} async-done(((bf16[128,512]{1,0:T(8,128)(2,1)}), bf16[2048,512]{1,0:T(8,128)(2,1)}) %all-gather.6.cloned.1.call-update) | async-done | bytes 2097168 | tf_op jit(solution)/shard_map/all_gather | solution.py:27
  96.7 2.0 multiply_convert_fusion.2
  98.8 40.3 %all-gather.8.cloned.1.call-done = bf16[2048,512]{1,0:T(8,128)(2,1)} async-done(((bf16[128,512]{1,0:T(8,128)(2,1)}), bf16[2048,512]{1,0:T(8,128)(2,1)}) %all-gather.8.cloned.1.call-update) | async-done | bytes 2097168 | tf_op jit(solution)/shard_map/all_gather | solution.py:31
  139.1 0.0 copy-start.1
  139.1 3.1 %convolution_convert_fusion = bf16[32,2048]{1,0:T(8,128)(2,1)} fusion(bf16[32,512]{1,0:T(8,128)(2,1)S(1)} %get-tuple-element.17, bf16[2048,512]{1,0:T(8,128)(2,1)} %all-gather.8.cloned.1.call-done), kind=kOutput, calls=%fused_computation.6 | convolution fusion | flops 67174400 | bytes 2260992 | tf_op jit(solution)/shard_map/dot_general | solution.py:32
  142.2 0.0 reduce-scatter.3.cloned.1.call-update
  142.3 0.0 reduce-scatter.5.cloned.1.call-start
  142.3 0.7 convolution_multiply_fusion
  143.1 0.0 copy-done.1
  143.1 0.5 fusion.20
  143.5 0.8 convolution_multiply_fusion.1
  144.3 0.8 convolution_multiply_fusion.2
  145.1 5.4 %pad_maximum_fusion = f32[2048,1536]{0,1:T(8,128)} fusion(f32[2048,512]{0,1:T(8,128)S(1)} %convolution_multiply_fusion, f32[2048,512]{0,1:T(8,128)S(1)} %convolution_multiply_fusion.1, f32[2048,512]{0,1:T(8,128)S(1)} %convolution_multiply_fusion.2), kind=kLoop, calls=%fused_computation | loop fusion | flops 6291456 | bytes 25165824 | tf_op jit(solution)/shard_map/concatenate | solution.py:64
  150.5 0.0 reduce-scatter.5.cloned.1.call-update
  150.5 1.0 reduce-scatter.3.cloned.1.call-done
  151.5 2.0 fusion
  153.5 136.7 %reduce-scatter.5.cloned.1.call-done = f32[128,1536]{0,1:T(8,128)} async-done(((f32[2048,1536]{0,1:T(8,128)}), f32[128,1536]{0,1:T(8,128)}) %reduce-scatter.5.cloned.1.call-update) | async-done | bytes 786448 | tf_op jit(solution)/shard_map/reduce_scatter | solution.py:63
  290.2 1.2 convert.6
  291.4 0.8 copy.19
  292.2 0.8 copy.18
  292.9 0.8 copy.17
  (3 shorter events, 0.1 us)
Async XLA Ops:
  7.2 12.9 %copy-start = (bf16[128,2048]{1,0:T(8,128)(2,1)S(1)}, bf16[128,2048]{1,0:T(8,128)(2,1)}, u32[]{:S(2)}) copy-start(bf16[128,2048]{1,0:T(8,128)(2,1)} %param.8) | copy-start | bytes 1572868
  7.2 47.2 %all-gather.4.cloned.1.call-start = ((), (), s32[]{:S(2)}) async-start(), calls=%async_computation.2 | async-start | bytes 2228224 | tf_op jit(solution)/shard_map/all_gather | solution.py:24
  7.9 88.8 %all-gather.6.cloned.1.call-start = ((), (), s32[]{:S(2)}) async-start(), calls=%async_computation.3 | async-start | bytes 2228224 | tf_op jit(solution)/shard_map/all_gather | solution.py:27
  8.7 130.4 %all-gather.8.cloned.1.call-start = ((), (), s32[]{:S(2)}) async-start(), calls=%async_computation.4 | async-start | bytes 2228224 | tf_op jit(solution)/shard_map/all_gather | solution.py:31
  9.4 142.1 %reduce-scatter.3.cloned.1.call-start = ((), (), s32[]{:S(2)}) async-start(), calls=%async_computation.5 | async-start | bytes 196608 | tf_op jit(solution)/shard_map/reduce_scatter | solution.py:33
  139.1 4.0 %copy-start.1 = (bf16[2048,512]{1,0:T(8,128)(2,1)S(1)}, bf16[2048,512]{1,0:T(8,128)(2,1)}, u32[]{:S(2)}) copy-start(bf16[2048,512]{1,0:T(8,128)(2,1)} %all-gather.8.cloned.1.call-done) | copy-start | bytes 6291460
  142.3 147.9 %reduce-scatter.5.cloned.1.call-start = ((), (), s32[]{:S(2)}) async-start(), calls=%async_computation.6 | async-start | bytes 13369344 | tf_op jit(solution)/shard_map/reduce_scatter | solution.py:63
Sparse Core Ops, SparseCore 0:
  10.2 44.1 all-gather.3
  56.5 40.1 all-gather.5
  98.9 40.1 all-gather.7
  142.4 9.0 reduce-scatter.2
  155.4 134.7 reduce-scatter.4
where the time goes:
time: 301 us; the launch traced here: 300 us
  waiting for transfers between devices  250 us (83%)
  between operations  14.5 us (5%)
  matrix products  13.7 us (5%)
  blocking collectives  10.8 us (4%)
  other arithmetic  8.91 us (3%)
    reduce_scatter x1, waiting for transfers between devices, per_device(): lax.psum_scatter(jnp.concatenate([term_of(picked, dgate), term_of(picked,...  137 us
    all_gather x1, waiting for transfers between devices, per_device(): full_down = lax.all_gather(w_down, 'dp', axis=0, tiled=True)  40.3 us
    all_gather x1, waiting for transfers between devices, per_device(): lax.all_gather(w_up, 'dp', axis=0, tiled=True)  40.3 us
    all_gather x1, waiting for transfers between devices, per_device(): lax.all_gather(w_gate, 'dp', axis=0, tiled=True)  29.2 us
  transfers between devices with their start and end apart: 5, of which 5 were waited for; matrix products, arithmetic and copies ran while one was open for 6% of the time, Pallas kernels for 0%

commit v1 on v0

--- a/solution.py
+++ b/solution.py
@@ -2,6 +2,27 @@
 import jax.numpy as jnp
 from jax import lax
 from jax.sharding import PartitionSpec as P
+
+
+def collect(shard, axis, dim):
+    peers, index, rows = (lax.axis_size(axis), lax.axis_index(axis), shard.shape[dim])
+    ahead = [(i, (i + 1) % peers) for i in range(peers)]
+    left = [(i, (i - 1) % peers) for i in range(peers)]
+    out = jnp.zeros((*shard.shape[:dim], peers * rows, *shard.shape[dim + 1 :]), shard.dtype)
+    out = lax.dynamic_update_slice_in_dim(out, shard, index * rows, axis=dim)
+    from_left = from_right = shard
+    half = peers // 2
+    for step in range(1, half + 1):
+        from_left = lax.ppermute(from_left, axis, ahead)
+        out = lax.dynamic_update_slice_in_dim(
+            out, from_left, (index - step) % peers * rows, axis=dim
+        )
+        if step < peers - half:
+            from_right = lax.ppermute(from_right, axis, left)
+            out = lax.dynamic_update_slice_in_dim(
+                out, from_right, (index + step) % peers * rows, axis=dim
+            )
+    return out
 
 
 def per_device(tokens, cotangent, expert_ids, route_weights, join_groups, w_gate, w_up, w_down):
@@ -20,9 +41,7 @@
         jnp.bfloat16
     )
     picked = lax.all_gather(picked_local, "expert", axis=0, tiled=True)
-    gate_acts = jnp.dot(
-        picked, lax.all_gather(w_gate, "dp", axis=0, tiled=True), preferred_element_type=jnp.float32
-    )
+    gate_acts = jnp.dot(picked, collect(w_gate, "dp", 0), preferred_element_type=jnp.float32)
     up_acts = jnp.dot(
         picked, lax.all_gather(w_up, "dp", axis=0, tiled=True), preferred_element_type=jnp.float32
     )

time: 301 us -> 262 us (0.87)
  waiting for transfers between devices: 250 us -> 181 us
  starting transfers between devices: 0.19 us -> 31.6 us
    all_gather x1, waiting for transfers between devices: 40.3 us -> 0.01 us  [per_device(): lax.all_gather(w_up, 'dp', axis=0, tiled=True)]
    ppermute x0 -> x15, starting transfers between devices: none -> 31.4 us  [the longest x7 31.4 us: collect(): from_right = lax.ppermute(from_right, axis, left)]
    ppermute x0 -> x15, waiting for transfers between devices: none -> 31 us  [the longest x8 20.7 us: collect(): from_left = lax.ppermute(from_left, axis, ahead)]
    all_gather x1 -> x0, waiting for transfers between devices: 29.2 us -> none  [per_device(): lax.all_gather(w_gate, 'dp', axis=0, tiled=True)]
    all_gather x1, waiting for transfers between devices: 40.3 us -> 11.7 us  [per_device(): full_down = lax.all_gather(w_down, 'dp', axis=0, tiled=True)]
  transfers between devices with their start and end apart: 5 -> 19, of which waited for: 5 -> 14; matrix products, arithmetic and copies ran while one was open for 6% -> 7% of each run, Pallas kernels for 0% -> 0%
where the time goes in v1:
time: 262 us
  waiting for transfers between devices  181 us (69%)
  starting transfers between devices  31.6 us (12%)
  between operations  14.7 us (6%)
  matrix products  12 us (5%)
  blocking collectives  9.86 us (4%)
  other arithmetic  8.94 us (3%)
  local copies, waits for them, and re-layouts  3.61 us (1%)
    reduce_scatter x1, waiting for transfers between devices, per_device(): lax.psum_scatter(jnp.concatenate([term_of(picked, dgate), term_of(picked,...  137 us
    ppermute x7, starting transfers between devices, collect(): from_right = lax.ppermute(from_right, axis, left)  31.4 us
    ppermute x8, waiting for transfers between devices, collect(): from_left = lax.ppermute(from_left, axis, ahead)  20.7 us
    all_gather x1, waiting for transfers between devices, per_device(): full_down = lax.all_gather(w_down, 'dp', axis=0, tiled=True)  11.7 us
    ppermute x7, waiting for transfers between devices, collect(): from_right = lax.ppermute(from_right, axis, left)  10.2 us
    concatenate x1, other arithmetic, per_device(): jnp.concatenate([term_of(picked, dgate), term_of(picked, dup), term_of(dp...  5.45 us
  transfers between devices with their start and end apart: 19, of which 14 were waited for; matrix products, arithmetic and copies ran while one was open for 7% of the time, Pallas kernels for 0%

profile of v1, /device:TPU:0, one launch (start us, length us, event | category | flops | bytes accessed | tf_op | source)
XLA Modules:
  0.0 261.5 jit_solution(13208961581520952991)
XLA Ops:
  7.2 0.7 all-gather.3.cloned.1.call-update
  8.0 0.7 all-gather.5.cloned.1.call-update
  8.7 5.5 %collective-permute-start.1 = (bf16[128,512]{1,0:T(8,128)(2,1)}, bf16[128,512]{1,0:T(8,128)(2,1)S(1)}, u32[]{:S(2)}, u32[]{:S(2)}) collective-permute-start(bf16[128,512]{1,0:T(8,128)(2,1)} %param.13), channel_id=1, source_target_pairs={{0,30},{2,0},{4,2},{6,4},{8,6},{10,8},{12,10},{14,12},{16,14},{18,... | collective-permute-start | bytes 393224 | tf_op jit(solution)/shard_map/ppermute | solution.py:21
  14.2 0.7 select_reduce_fusion
  15.0 0.1 copy.16
  15.1 0.2 reduce-window.8
  15.3 0.1 add_reduce_fusion
  15.4 1.6 convolution_convert_fusion.1
  17.0 4.9 %all_gather.15 = bf16[32,2048]{1,0:T(8,128)(2,1)S(1)} all-gather(bf16[16,2048]{1,0:T(8,128)(2,1)S(1)} %convolution_convert_fusion.1), channel_id=1, replica_groups=mesh['dp'=16,'expert'=2] {'expert'}, dimensions={0}, use_global_device_ids=true | all-gather | bytes 196608 | tf_op jit(solution)/shard_map/all_gather | solution.py:67
  21.9 1.3 fusion.15
  23.2 0.2 convolution_convert_fusion.2
  23.4 4.9 %all_gather.12 = bf16[32,2048]{1,0:T(8,128)(2,1)S(1)} all-gather(bf16[16,2048]{1,0:T(8,128)(2,1)S(1)} %convolution_convert_fusion.2), channel_id=1, replica_groups=mesh['dp'=16,'expert'=2] {'expert'}, dimensions={0}, use_global_device_ids=true | all-gather | bytes 196608 | tf_op jit(solution)/shard_map/all_gather | solution.py:43
  29.1 0.1 broadcast_in_dim.16
  29.2 2.6 collective-permute-start.3
  31.9 2.5 collective-permute-done.3
  34.4 4.7 %collective-permute-start.5 = (bf16[128,512]{1,0:T(8,128)(2,1)S(1)}, bf16[128,512]{1,0:T(8,128)(2,1)S(1)}, u32[]{:S(2)}, u32[]{:S(2)}) collective-permute-start(bf16[128,512]{1,0:T(8,128)(2,1)S(1)} %collective-permute-done.3), channel_id=1, source_target_pairs={{0,30},{2,0},{4,2},{6,4},{8,6},{10,8},{12,10},{14,12},{16,14},{18,... | collective-permute-start | bytes 393224 | tf_op jit(solution)/shard_map/ppermute | solution.py:21
  39.1 3.5 %collective-permute-done.5 = bf16[128,512]{1,0:T(8,128)(2,1)S(1)} collective-permute-done((bf16[128,512]{1,0:T(8,128)(2,1)S(1)}, bf16[128,512]{1,0:T(8,128)(2,1)S(1)}, u32[]{:S(2)}, u32[]{:S(2)}) %collective-permute-start.5) | collective-permute-done | bytes 131104 | tf_op jit(solution)/shard_map/ppermute | solution.py:21
  42.6 4.7 %collective-permute-start.7 = (bf16[128,512]{1,0:T(8,128)(2,1)S(1)}, bf16[128,512]{1,0:T(8,128)(2,1)S(1)}, u32[]{:S(2)}, u32[]{:S(2)}) collective-permute-start(bf16[128,512]{1,0:T(8,128)(2,1)S(1)} %collective-permute-done.5), channel_id=1, source_target_pairs={{0,30},{2,0},{4,2},{6,4},{8,6},{10,8},{12,10},{14,12},{16,14},{18,... | collective-permute-start | bytes 393224 | tf_op jit(solution)/shard_map/ppermute | solution.py:21
  47.3 1.0 collective-permute-done.4
  48.3 2.6 %collective-permute-done.7 = bf16[128,512]{1,0:T(8,128)(2,1)S(1)} collective-permute-done((bf16[128,512]{1,0:T(8,128)(2,1)S(1)}, bf16[128,512]{1,0:T(8,128)(2,1)S(1)}, u32[]{:S(2)}, u32[]{:S(2)}) %collective-permute-start.7) | collective-permute-done | bytes 131104 | tf_op jit(solution)/shard_map/ppermute | solution.py:21
  50.9 4.6 %collective-permute-start.9 = (bf16[128,512]{1,0:T(8,128)(2,1)S(1)}, bf16[128,512]{1,0:T(8,128)(2,1)S(1)}, u32[]{:S(2)}, u32[]{:S(2)}) collective-permute-start(bf16[128,512]{1,0:T(8,128)(2,1)S(1)} %collective-permute-done.7), channel_id=1, source_target_pairs={{0,30},{2,0},{4,2},{6,4},{8,6},{10,8},{12,10},{14,12},{16,14},{18,... | collective-permute-start | bytes 393224 | tf_op jit(solution)/shard_map/ppermute | solution.py:21
  55.5 1.7 collective-permute-done.6
  57.3 0.8 collective-permute-done.9
  58.1 4.7 %collective-permute-start.11 = (bf16[128,512]{1,0:T(8,128)(2,1)S(1)}, bf16[128,512]{1,0:T(8,128)(2,1)S(1)}, u32[]{:S(2)}, u32[]{:S(2)}) collective-permute-start(bf16[128,512]{1,0:T(8,128)(2,1)S(1)} %collective-permute-done.9), channel_id=1, source_target_pairs={{0,30},{2,0},{4,2},{6,4},{8,6},{10,8},{12,10},{14,12},{16,14},{18,... | collective-permute-start | bytes 393224 | tf_op jit(solution)/shard_map/ppermute | solution.py:21
  62.7 1.7 collective-permute-done.8
  64.5 0.8 collective-permute-done.11
  65.2 4.7 %collective-permute-start.13 = (bf16[128,512]{1,0:T(8,128)(2,1)S(1)}, bf16[128,512]{1,0:T(8,128)(2,1)S(1)}, u32[]{:S(2)}, u32[]{:S(2)}) collective-permute-start(bf16[128,512]{1,0:T(8,128)(2,1)S(1)} %collective-permute-done.11), channel_id=1, source_target_pairs={{0,30},{2,0},{4,2},{6,4},{8,6},{10,8},{12,10},{14,12},{16,14},{18,... | collective-permute-start | bytes 393224 | tf_op jit(solution)/shard_map/ppermute | solution.py:21
  69.9 1.7 collective-permute-done.10
  71.7 7.6 %collective-permute-done.12 = bf16[128,512]{1,0:T(8,128)(2,1)S(1)} collective-permute-done((bf16[128,512]{1,0:T(8,128)(2,1)S(1)}, bf16[128,512]{1,0:T(8,128)(2,1)S(1)}, u32[]{:S(2)}, u32[]{:S(2)}) %collective-permute-start.12) | collective-permute-done | bytes 131104 | tf_op jit(solution)/shard_map/ppermute | solution.py:16
  79.3 7.1 %collective-permute-done.14 = bf16[128,512]{1,0:T(8,128)(2,1)S(1)} collective-permute-done((bf16[128,512]{1,0:T(8,128)(2,1)S(1)}, bf16[128,512]{1,0:T(8,128)(2,1)S(1)}, u32[]{:S(2)}, u32[]{:S(2)}) %collective-permute-start.14) | collective-permute-done | bytes 131104 | tf_op jit(solution)/shard_map/ppermute | solution.py:16
  86.4 0.5 fusion.19
  86.9 2.1 multiply_convert_fusion.2
  88.9 11.7 %all-gather.5.cloned.1.call-done = bf16[2048,512]{1,0:T(8,128)(2,1)} async-done(((bf16[128,512]{1,0:T(8,128)(2,1)}), bf16[2048,512]{1,0:T(8,128)(2,1)}) %all-gather.5.cloned.1.call-update) | async-done | bytes 2097168 | tf_op jit(solution)/shard_map/all_gather | solution.py:50
  100.6 3.0 %convolution_convert_fusion = bf16[32,2048]{1,0:T(8,128)(2,1)} fusion(bf16[32,512]{1,0:T(8,128)(2,1)S(1)} %get-tuple-element.17, bf16[2048,512]{1,0:T(8,128)(2,1)} %all-gather.5.cloned.1.call-done), kind=kOutput, calls=%fused_computation.6 | convolution fusion | flops 67174400 | bytes 2260992 | tf_op jit(solution)/shard_map/dot_general | solution.py:51
  103.6 0.0 reduce-scatter.5.cloned.1.call-start
  103.6 0.7 convolution_multiply_fusion
  104.4 0.8 copy-done.1
  105.2 0.4 fusion.20
  105.6 0.8 convolution_multiply_fusion.1
  106.4 0.8 convolution_multiply_fusion.2
  107.2 5.4 %pad_maximum_fusion = f32[2048,1536]{0,1:T(8,128)} fusion(f32[2048,512]{0,1:T(8,128)S(1)} %convolution_multiply_fusion, f32[2048,512]{0,1:T(8,128)S(1)} %convolution_multiply_fusion.1, f32[2048,512]{0,1:T(8,128)S(1)} %convolution_multiply_fusion.2), kind=kLoop, calls=%fused_computation | loop fusion | flops 6291456 | bytes 25165824 | tf_op jit(solution)/shard_map/concatenate | solution.py:83
  112.6 0.2 reduce-scatter.3.cloned.1.call-done
  112.8 2.0 fusion
  114.8 136.7 %reduce-scatter.5.cloned.1.call-done = f32[128,1536]{0,1:T(8,128)} async-done(((f32[2048,1536]{0,1:T(8,128)}), f32[128,1536]{0,1:T(8,128)}) %reduce-scatter.5.cloned.1.call-update) | async-done | bytes 786448 | tf_op jit(solution)/shard_map/reduce_scatter | solution.py:82
  251.5 1.2 convert.6
  252.7 0.8 copy.19
  253.5 0.8 copy.18
  254.2 0.8 copy.17
  (42 shorter events, 0.5 us)
Async XLA Ops:
  7.2 16.1 %copy-start = (bf16[128,2048]{1,0:T(8,128)(2,1)S(1)}, bf16[128,2048]{1,0:T(8,128)(2,1)}, u32[]{:S(2)}) copy-start(bf16[128,2048]{1,0:T(8,128)(2,1)} %param.8) | copy-start | bytes 1572868
  7.2 79.7 %all-gather.3.cloned.1.call-start = ((), (), s32[]{:S(2)}) async-start(), calls=%async_computation.2 | async-start | bytes 2228224 | tf_op jit(solution)/shard_map/all_gather | solution.py:46
  7.9 92.7 %all-gather.5.cloned.1.call-start = ((), (), s32[]{:S(2)}) async-start(), calls=%async_computation.3 | async-start | bytes 2228224 | tf_op jit(solution)/shard_map/all_gather | solution.py:50
  8.7 104.1 %reduce-scatter.3.cloned.1.call-start = ((), (), s32[]{:S(2)}) async-start(), calls=%async_computation.4 | async-start | bytes 196608 | tf_op jit(solution)/shard_map/reduce_scatter | solution.py:52
  8.7 20.5 %collective-permute-start.1 = (bf16[128,512]{1,0:T(8,128)(2,1)}, bf16[128,512]{1,0:T(8,128)(2,1)S(1)}, u32[]{:S(2)}, u32[]{:S(2)}) collective-permute-start(bf16[128,512]{1,0:T(8,128)(2,1)} %param.13), channel_id=1, source_target_pairs={{0,30},{2,0},{4,2},{6,4},{8,6},{10,8},{12,10},{14,12},{16,14},{18,... | collective-permute-start | bytes 393224 | tf_op jit(solution)/shard_map/ppermute | solution.py:21
  14.2 17.6 %collective-permute-start = (bf16[128,512]{1,0:T(8,128)(2,1)}, bf16[128,512]{1,0:T(8,128)(2,1)S(1)}, u32[]{:S(2)}, u32[]{:S(2)}) collective-permute-start(bf16[128,512]{1,0:T(8,128)(2,1)} %param.13), channel_id=1, source_target_pairs={{0,2},{2,4},{4,6},{6,8},{8,10},{10,12},{12,14},{14,16},{16,18},{18... | collective-permute-start | bytes 393224 | tf_op jit(solution)/shard_map/ppermute | solution.py:16
  15.3 13.9 %copy-start.2 = (bf16[128,512]{1,0:T(8,128)(2,1)S(1)}, bf16[128,512]{1,0:T(8,128)(2,1)}, u32[]{:S(2)}) copy-start(bf16[128,512]{1,0:T(8,128)(2,1)} %param.13) | copy-start | bytes 393220
  29.2 5.1 %collective-permute-start.3 = (bf16[128,512]{1,0:T(8,128)(2,1)S(1)}, bf16[128,512]{1,0:T(8,128)(2,1)S(1)}, u32[]{:S(2)}, u32[]{:S(2)}) collective-permute-start(bf16[128,512]{1,0:T(8,128)(2,1)S(1)} %collective-permute-done.1), channel_id=1, source_target_pairs={{0,30},{2,0},{4,2},{6,4},{8,6},{10,8},{12,10},{14,12},{16,14},{18,... | collective-permute-start | bytes 393224 | tf_op jit(solution)/shard_map/ppermute | solution.py:21
  31.8 7.2 %collective-permute-start.2 = (bf16[128,512]{1,0:T(8,128)(2,1)S(1)}, bf16[128,512]{1,0:T(8,128)(2,1)S(1)}, u32[]{:S(2)}, u32[]{:S(2)}) collective-permute-start(bf16[128,512]{1,0:T(8,128)(2,1)S(1)} %collective-permute-done), channel_id=1, source_target_pairs={{0,2},{2,4},{4,6},{6,8},{8,10},{10,12},{12,14},{14,16},{16,18},{18... | collective-permute-start | bytes 393224 | tf_op jit(solution)/shard_map/ppermute | solution.py:16
  34.4 8.2 %collective-permute-start.5 = (bf16[128,512]{1,0:T(8,128)(2,1)S(1)}, bf16[128,512]{1,0:T(8,128)(2,1)S(1)}, u32[]{:S(2)}, u32[]{:S(2)}) collective-permute-start(bf16[128,512]{1,0:T(8,128)(2,1)S(1)} %collective-permute-done.3), channel_id=1, source_target_pairs={{0,30},{2,0},{4,2},{6,4},{8,6},{10,8},{12,10},{14,12},{16,14},{18,... | collective-permute-start | bytes 393224 | tf_op jit(solution)/shard_map/ppermute | solution.py:21
  39.0 9.2 %collective-permute-start.4 = (bf16[128,512]{1,0:T(8,128)(2,1)S(1)}, bf16[128,512]{1,0:T(8,128)(2,1)S(1)}, u32[]{:S(2)}, u32[]{:S(2)}) collective-permute-start(bf16[128,512]{1,0:T(8,128)(2,1)S(1)} %collective-permute-done.2), channel_id=1, source_target_pairs={{0,2},{2,4},{4,6},{6,8},{8,10},{10,12},{12,14},{14,16},{16,18},{18... | collective-permute-start | bytes 393224 | tf_op jit(solution)/shard_map/ppermute | solution.py:16
  42.6 8.3 %collective-permute-start.7 = (bf16[128,512]{1,0:T(8,128)(2,1)S(1)}, bf16[128,512]{1,0:T(8,128)(2,1)S(1)}, u32[]{:S(2)}, u32[]{:S(2)}) collective-permute-start(bf16[128,512]{1,0:T(8,128)(2,1)S(1)} %collective-permute-done.5), channel_id=1, source_target_pairs={{0,30},{2,0},{4,2},{6,4},{8,6},{10,8},{12,10},{14,12},{16,14},{18,... | collective-permute-start | bytes 393224 | tf_op jit(solution)/shard_map/ppermute | solution.py:21
  48.2 9.0 %collective-permute-start.6 = (bf16[128,512]{1,0:T(8,128)(2,1)S(1)}, bf16[128,512]{1,0:T(8,128)(2,1)S(1)}, u32[]{:S(2)}, u32[]{:S(2)}) collective-permute-start(bf16[128,512]{1,0:T(8,128)(2,1)S(1)} %collective-permute-done.4), channel_id=1, source_target_pairs={{0,2},{2,4},{4,6},{6,8},{8,10},{10,12},{12,14},{14,16},{16,18},{18... | collective-permute-start | bytes 393224 | tf_op jit(solution)/shard_map/ppermute | solution.py:16
  50.9 7.1 %collective-permute-start.9 = (bf16[128,512]{1,0:T(8,128)(2,1)S(1)}, bf16[128,512]{1,0:T(8,128)(2,1)S(1)}, u32[]{:S(2)}, u32[]{:S(2)}) collective-permute-start(bf16[128,512]{1,0:T(8,128)(2,1)S(1)} %collective-permute-done.7), channel_id=1, source_target_pairs={{0,30},{2,0},{4,2},{6,4},{8,6},{10,8},{12,10},{14,12},{16,14},{18,... | collective-permute-start | bytes 393224 | tf_op jit(solution)/shard_map/ppermute | solution.py:21
  57.2 7.2 %collective-permute-start.8 = (bf16[128,512]{1,0:T(8,128)(2,1)S(1)}, bf16[128,512]{1,0:T(8,128)(2,1)S(1)}, u32[]{:S(2)}, u32[]{:S(2)}) collective-permute-start(bf16[128,512]{1,0:T(8,128)(2,1)S(1)} %collective-permute-done.6), channel_id=1, source_target_pairs={{0,2},{2,4},{4,6},{6,8},{8,10},{10,12},{12,14},{14,16},{16,18},{18... | collective-permute-start | bytes 393224 | tf_op jit(solution)/shard_map/ppermute | solution.py:16
  58.1 7.2 %collective-permute-start.11 = (bf16[128,512]{1,0:T(8,128)(2,1)S(1)}, bf16[128,512]{1,0:T(8,128)(2,1)S(1)}, u32[]{:S(2)}, u32[]{:S(2)}) collective-permute-start(bf16[128,512]{1,0:T(8,128)(2,1)S(1)} %collective-permute-done.9), channel_id=1, source_target_pairs={{0,30},{2,0},{4,2},{6,4},{8,6},{10,8},{12,10},{14,12},{16,14},{18,... | collective-permute-start | bytes 393224 | tf_op jit(solution)/shard_map/ppermute | solution.py:21
  64.4 7.2 %collective-permute-start.10 = (bf16[128,512]{1,0:T(8,128)(2,1)S(1)}, bf16[128,512]{1,0:T(8,128)(2,1)S(1)}, u32[]{:S(2)}, u32[]{:S(2)}) collective-permute-start(bf16[128,512]{1,0:T(8,128)(2,1)S(1)} %collective-permute-done.8), channel_id=1, source_target_pairs={{0,2},{2,4},{4,6},{6,8},{8,10},{10,12},{12,14},{14,16},{16,18},{18... | collective-permute-start | bytes 393224 | tf_op jit(solution)/shard_map/ppermute | solution.py:16
  65.2 14.0 %collective-permute-start.13 = (bf16[128,512]{1,0:T(8,128)(2,1)S(1)}, bf16[128,512]{1,0:T(8,128)(2,1)S(1)}, u32[]{:S(2)}, u32[]{:S(2)}) collective-permute-start(bf16[128,512]{1,0:T(8,128)(2,1)S(1)} %collective-permute-done.11), channel_id=1, source_target_pairs={{0,30},{2,0},{4,2},{6,4},{8,6},{10,8},{12,10},{14,12},{16,14},{18,... | collective-permute-start | bytes 393224 | tf_op jit(solution)/shard_map/ppermute | solution.py:21
  71.7 7.6 %collective-permute-start.12 = (bf16[128,512]{1,0:T(8,128)(2,1)S(1)}, bf16[128,512]{1,0:T(8,128)(2,1)S(1)}, u32[]{:S(2)}, u32[]{:S(2)}) collective-permute-start(bf16[128,512]{1,0:T(8,128)(2,1)S(1)} %collective-permute-done.10), channel_id=1, source_target_pairs={{0,2},{2,4},{4,6},{6,8},{8,10},{10,12},{12,14},{14,16},{16,18},{18... | collective-permute-start | bytes 393224 | tf_op jit(solution)/shard_map/ppermute | solution.py:16
  79.3 7.1 %collective-permute-start.14 = (bf16[128,512]{1,0:T(8,128)(2,1)S(1)}, bf16[128,512]{1,0:T(8,128)(2,1)S(1)}, u32[]{:S(2)}, u32[]{:S(2)}) collective-permute-start(bf16[128,512]{1,0:T(8,128)(2,1)S(1)} %collective-permute-done.12), channel_id=1, source_target_pairs={{0,2},{2,4},{4,6},{6,8},{8,10},{10,12},{12,14},{14,16},{16,18},{18... | collective-permute-start | bytes 393224 | tf_op jit(solution)/shard_map/ppermute | solution.py:16
  103.6 1.6 copy-start.1
  103.6 147.9 %reduce-scatter.5.cloned.1.call-start = ((), (), s32[]{:S(2)}) async-start(), calls=%async_computation.5 | async-start | bytes 13369344 | tf_op jit(solution)/shard_map/reduce_scatter | solution.py:82
Sparse Core Ops, SparseCore 0:
  10.2 46.1 all-gather.2
  58.6 41.9 all-gather.4
  103.7 9.0 reduce-scatter.2
  116.7 134.7 reduce-scatter.4
